TPU v7x, 512 devices: a whole 4x4x16 slice. The times are simulated.
512 devices in a mesh: domain: 64 (over x, y, z_lo), member: 8 (over z_hi, core).
Axes of the slice: x: 4, y: 4, z: 16 (z_hi: 4, z_lo: 4; z = z_hi * 4 + z_lo), core: 2. Of those that a mesh axis runs over, the one named last changes fastest.
Arguments:
- inputs: bfloat16 [16, 12288, 1024], P('member', 'domain')
- norm_gain: bfloat16 [1024], P('member'), may hold values from 0.099609375 to 1.8984375
- w_query: bfloat16 [1024, 512], P('member')
- w_key: bfloat16 [1024, 512], P('member')
- w_value: bfloat16 [1024, 512], P('member'), may hold values from -0.1875 to 0.1875
- w_out: bfloat16 [512, 1024], P('member'), may hold values from -0.75 to 0.75
- neighbors: int32 [192, 9], P('domain'), may hold values from 0 to 191, as said below
- slot_valid: int32 [192, 9], P('domain'), may hold values from 0 to 1, as said below
- output_cotangent: bfloat16 [16, 12288, 1024], P('member', 'domain'), may hold values from -1.5 to 1.5
Outputs:
- attn_out: bfloat16 [16, 12288, 1024], P('member', 'domain')
- d_input: bfloat16 [16, 12288, 1024], P('member', 'domain')
- grad_wout: float32 [512, 1024], P('member')
Inputs may be any that keep to these rules, and one draw needn't show every extreme that they name: `neighbors`: slot 0 of block b names b. The blocks named by the valid slots of b are distinct and lie within blocks (b // 3 - 1) * 3 to (b // 3 + 2) * 3 - 1. An invalid slot names b. `slot_valid`: slot 0 is always 1.
All inputs are finite; a program needn't handle non-finite values.
Results may differ from a plain program's by a relative error of at most 0.019.
Values may be sent and summed in bfloat16 or wider, within the bound.
No kernel may reach another device: no remote copies, remote signals or barrier semaphores. Data moves between devices by JAX's collectives and lax.ppermute only.
A program may use at most 128 MiB of HBM per device.

v0:
```python
import jax
import jax.numpy as jnp
from jax import lax
from jax.sharding import PartitionSpec as P

HEAD_DIM = 64
EPSILON = 1e-06
MASKED = -1e30


def extended_2(value, sides, width):
    for axis, dim in sides:
        peers, length = (lax.axis_size(axis), value.shape[dim])
        up = [(i, (i + 1) % peers) for i in range(peers - 1)]
        down = [(j, i) for i, j in up]
        last = lax.slice_in_dim(value, length - width, length, axis=dim)
        initial = lax.slice_in_dim(value, 0, width, axis=dim)
        before = lax.ppermute(last, axis, up)
        after = lax.ppermute(initial, axis, down)
        value = jnp.concatenate([before, value, after], axis=dim)
    return value


def pair_columns(field, pair_index, pair_width):
    return lax.dynamic_slice_in_dim(field, pair_index * pair_width, pair_width, field.ndim - 1)


def shards(
    inputs, norm_gain, w_query, w_key, w_value, w_out, neighbors, slot_valid, output_cotangent
):
    samples, length, model_width = inputs.shape
    block_count, slot_count = neighbors.shape
    block_len = length // block_count
    window_blocks = 3 * block_count
    full_gain, complete_query, complete_key, complete_value, complete_output = (
        lax.all_gather(norm_gain, "member", axis=0, tiled=True),
        lax.all_gather(w_query, "member", axis=0, tiled=True),
        lax.all_gather(w_key, "member", axis=0, tiled=True),
        lax.all_gather(w_value, "member", axis=0, tiled=True),
        lax.all_gather(w_out, "member", axis=0, tiled=True),
    )
    hidden_width = complete_query.shape[1]
    pair_width = 2 * HEAD_DIM
    pair_count = hidden_width // pair_width
    score_scale = HEAD_DIM ** (-0.5)
    inputs_float = inputs.astype(jnp.float32)
    inverse_rms = lax.rsqrt(jnp.mean(inputs_float * inputs_float, axis=-1, keepdims=True) + EPSILON)
    gain_float = full_gain.astype(jnp.float32)
    normalized_input = (inputs_float * inverse_rms * gain_float).astype(jnp.bfloat16)
    query = jnp.einsum(
        "fbi,iy->fby", normalized_input, complete_query, preferred_element_type=jnp.float32
    ).astype(jnp.bfloat16)
    key_rows = jnp.einsum(
        "fbi,iy->fby", normalized_input, complete_key, preferred_element_type=jnp.float32
    ).astype(jnp.bfloat16)
    value_rows = jnp.einsum(
        "fbi,iy->fby", normalized_input, complete_value, preferred_element_type=jnp.float32
    ).astype(jnp.bfloat16)
    key_value = jnp.concatenate([key_rows, value_rows], axis=-1)
    extended = extended_2(key_value, (("domain", 1),), length)
    domain_rank = lax.axis_index("domain")
    local_index = neighbors - (domain_rank - 1) * block_count
    present = slot_valid > 0
    window_ids = jnp.arange(window_blocks, dtype=jnp.int32)
    key_all = extended[..., :hidden_width]
    value_all = extended[..., hidden_width:]
    score_spec = "sbqgd,skgd->sbgqk"
    mix_spec = "sbgqk,skgd->sbqgd"
    back_spec = "sbgqk,sbqgd->skgd"
    matches = jnp.logical_and(
        local_index[:, :, None] == window_ids[None, None, :], present[:, :, None]
    )
    included = jnp.any(matches, axis=1)
    key_mask = jnp.repeat(included, block_len, axis=1)

    def pair_keys(pair_index):
        key_pair = pair_columns(key_all, pair_index, pair_width).reshape(
            samples, window_blocks * block_len, 2, HEAD_DIM
        )
        value_pair = pair_columns(value_all, pair_index, pair_width).reshape(
            samples, window_blocks * block_len, 2, HEAD_DIM
        )
        return (key_pair, value_pair)

    def to_window(grad_keys):
        return grad_keys.reshape(samples, window_blocks * block_len, pair_width)

    def pair_probability(pair_index):
        query_pair = pair_columns(query, pair_index, pair_width).reshape(
            samples, block_count, block_len, 2, HEAD_DIM
        )
        key_pair, value_pair = pair_keys(pair_index)
        scores = (
            jnp.einsum(score_spec, query_pair, key_pair, preferred_element_type=jnp.float32)
            * score_scale
        )
        scores = jnp.where(key_mask[None, :, None, None, :], scores, MASKED)
        row_max = jnp.max(scores, axis=-1, keepdims=True)
        shifted = jnp.exp(scores - row_max)
        probability = shifted / jnp.sum(shifted, axis=-1, keepdims=True)
        return (query_pair, key_pair, value_pair, probability)

    def forward_pair(pair_index):
        query_pair, key_pair, value_pair, probability = pair_probability(pair_index)
        prob_bf = probability.astype(jnp.bfloat16)
        mixed_pair = jnp.einsum(mix_spec, prob_bf, value_pair, preferred_element_type=jnp.float32)
        return mixed_pair.astype(jnp.bfloat16).reshape(samples, length, pair_width)

    attention_pairs = lax.map(forward_pair, jnp.arange(pair_count))
    neighbour_attention = jnp.transpose(attention_pairs, (1, 2, 0, 3)).reshape(
        samples, length, hidden_width
    )
    attn_out = jnp.einsum(
        "qny,yb->qnb", neighbour_attention, complete_output, preferred_element_type=jnp.float32
    ).astype(jnp.bfloat16)
    d_attention = jnp.einsum(
        "yjz,bz->yjb", output_cotangent, complete_output, preferred_element_type=jnp.float32
    ).astype(jnp.bfloat16)
    row_share = hidden_width // lax.axis_size("member")
    member_total = samples * lax.axis_size("member")
    incomplete_gradient = jnp.einsum(
        "rfe,rfu->eu", neighbour_attention, output_cotangent, preferred_element_type=jnp.float32
    )
    total_grad = lax.psum(incomplete_gradient, ("domain", "member"))
    grad_mine = lax.dynamic_slice_in_dim(
        total_grad, lax.axis_index("member") * row_share, row_share, 0
    )
    grad_wout = grad_mine / member_total

    def backward_pair(pair_index):
        query_pair, key_pair, value_pair, probability = pair_probability(pair_index)
        prob_bf = probability.astype(jnp.bfloat16)
        grad_pair = pair_columns(d_attention, pair_index, pair_width).reshape(
            samples, block_count, block_len, 2, HEAD_DIM
        )
        d_prob = jnp.einsum(score_spec, grad_pair, value_pair, preferred_element_type=jnp.float32)
        delta = jnp.sum(probability * d_prob, axis=-1, keepdims=True)
        d_score = (probability * (d_prob - delta) * score_scale).astype(jnp.bfloat16)
        d_query_pair = jnp.einsum(mix_spec, d_score, key_pair, preferred_element_type=jnp.float32)
        d_query_pair = d_query_pair.astype(jnp.bfloat16).reshape(samples, length, pair_width)
        d_key_pair = jnp.einsum(back_spec, d_score, query_pair, preferred_element_type=jnp.float32)
        d_value_pair = jnp.einsum(back_spec, prob_bf, grad_pair, preferred_element_type=jnp.float32)
        return (d_query_pair, to_window(d_key_pair), to_window(d_value_pair))

    query_grads, key_grads, value_grads = lax.map(backward_pair, jnp.arange(pair_count))
    query_cotangent = jnp.transpose(query_grads, (1, 2, 0, 3)).reshape(
        samples, length, hidden_width
    )
    key_ext = jnp.transpose(key_grads, (1, 2, 0, 3)).reshape(samples, 3 * length, hidden_width)
    value_ext = jnp.transpose(value_grads, (1, 2, 0, 3)).reshape(samples, 3 * length, hidden_width)
    ext_grad = jnp.concatenate([key_ext, value_ext], axis=-1)
    lower_rim = ext_grad[:, :length]
    own_part = ext_grad[:, length : 2 * length]
    upper_rim = ext_grad[:, 2 * length :]
    rims_half = jnp.concatenate([lower_rim, upper_rim], axis=1).astype(jnp.bfloat16)
    returned = extended_2(rims_half, (("domain", 1),), length)
    from_below = returned[:, :length].astype(jnp.float32)
    from_above = returned[:, 3 * length :].astype(jnp.float32)
    kv_total = own_part + from_below + from_above
    kv_grad = kv_total.astype(jnp.bfloat16)
    key_cotangent = kv_grad[..., :hidden_width]
    value_cotangent = kv_grad[..., hidden_width:]
    normed_cotangent = jnp.einsum(
        "qja,ga->qjg", query_cotangent, complete_query, preferred_element_type=jnp.float32
    )
    normed_cotangent = normed_cotangent + jnp.einsum(
        "qja,ga->qjg", key_cotangent, complete_key, preferred_element_type=jnp.float32
    )
    normed_cotangent = normed_cotangent + jnp.einsum(
        "qja,ga->qjg", value_cotangent, complete_value, preferred_element_type=jnp.float32
    )
    scaled_grad = normed_cotangent * gain_float
    inner_mean = jnp.mean(scaled_grad * inputs_float, axis=-1, keepdims=True)
    d_input = inverse_rms * scaled_grad - inputs_float * inverse_rms**3 * inner_mean
    return (attn_out, d_input.astype(jnp.bfloat16), grad_wout)


def solution(mesh):
    placed = (
        P("member", "domain", None),
        P("member"),
        P("member", None),
        P("member", None),
        P("member", None),
        P("member", None),
        P("domain", None),
        P("domain", None),
        P("member", "domain", None),
    )
    return jax.shard_map(
        shards,
        mesh=mesh,
        in_specs=placed,
        out_specs=(P("member", "domain", None), P("member", "domain", None), P("member", None)),
        check_vma=False,
    )
```

profile of v0, /device:TPU:1, one launch (start us, length us, event | category | flops | bytes accessed | tf_op | source)
XLA Modules:
  0.0 901.7 jit_solution(3319372591805515954)
XLA Ops:
  11.5 22.8 %all-gather = bf16[8,1,128]{2,1,0:T(2,128)(2,1)S(1)} all-gather(bf16[1,1,128]{2,1,0:T(2,128)(2,1)} %bitcast.205), channel_id=1, replica_groups=mesh['domain'=64,'member'=8] {'member'}, dimensions={0}, use_global_device_ids=true | all-gather | bytes 2304 | tf_op jit(solution)/shard_map/all_gather | solution.py:36
  35.0 28.1 %all-gather.8.cloned.1.call-done = bf16[1024,512]{1,0:T(8,128)(2,1)} async-done(((bf16[128,512]{1,0:T(8,128)(2,1)}), bf16[1024,512]{1,0:T(8,128)(2,1)}) %all-gather.8.cloned.1.call-update) | async-done | bytes 1048592 | tf_op jit(solution)/shard_map/all_gather | solution.py:39
  65.2 42.2 %all-gather.6.cloned.1.call-done = bf16[1024,512]{1,0:T(8,128)(2,1)} async-done(((bf16[128,512]{1,0:T(8,128)(2,1)}), bf16[1024,512]{1,0:T(8,128)(2,1)}) %all-gather.6.cloned.1.call-update) | async-done | bytes 1048592 | tf_op jit(solution)/shard_map/all_gather | solution.py:38
  111.5 4.9 collective-permute-start
  116.7 37.4 %all-gather.12.cloned.1.call-done = bf16[512,1024]{1,0:T(8,128)(2,1)} async-done(((bf16[64,1024]{1,0:T(8,128)(2,1)}), bf16[512,1024]{1,0:T(8,128)(2,1)}) %all-gather.12.cloned.1.call-update) | async-done | bytes 1048592 | tf_op jit(solution)/shard_map/all_gather | solution.py:40
  156.6 59.6 %all-gather.10.cloned.1.call-done = bf16[1024,512]{1,0:T(8,128)(2,1)} async-done(((bf16[128,512]{1,0:T(8,128)(2,1)}), bf16[1024,512]{1,0:T(8,128)(2,1)}) %all-gather.10.cloned.1.call-update) | async-done | bytes 1048592 | tf_op jit(solution)/shard_map/all_gather | solution.py:37
  224.2 34.7 %while.26 = (s32[]{:T(128)}, bf16[4,2,192,128]{3,2,1,0:T(8,128)(2,1)}, s32[4]{0:T(128)S(1)}, bf16[2,576,512]{1,2,0:T(8,128)(2,1)}, bf16[2,576,512]{1,2,0:T(8,128...) while((s32[]{:T(128)}, ...), condition=%wide.region_5.6_spmd.clone, body=%wide.region_2.5_spmd.clone.sunk | while | flops 117278592 | bytes 8469142 | solution.py:109
  259.7 121.8 %while.27 = (s32[]{:T(128)}, bf16[4,2,192,128]{3,2,1,0:T(8,128)(2,1)}, f32[4,2,576,128]{2,3,1,0:T(8,128)}, f32[4,2,576,128]{2,3,1,0:T(8,128)}, s32[4]{0:T(128)S(...) while((s32[]{:T(128)}, ...), condition=%wide.region_10.11_spmd.clone, body=%wide.region_6.0_spmd.clone.sunk | while | flops 293343744 | bytes 26301140 | solution.py:145
  269.1 7.8 fusion.143
  281.2 7.7 fusion.145
  299.5 7.8 fusion.143
  311.6 7.7 fusion.145
  329.9 7.8 fusion.143
  342.0 7.7 fusion.145
  360.4 7.8 fusion.143
  372.5 7.7 fusion.145
  381.4 3.2 copy.65
  386.8 3.5 constant_dynamic-update-slice_fusion.5
  392.8 2.7 reshape.82
  397.3 2.7 convert.6
  402.3 4.9 collective-permute-start.2
  409.3 2.8 convolution_convert_fusion.1
  412.7 9.3 %collective-permute-done.3 = bf16[2,192,1024]{2,1,0:T(8,128)(2,1)} collective-permute-done((bf16[2,192,1024]{2,1,0:T(8,128)(2,1)}, bf16[2,192,1024]{2,1,0:T(8,128)(2,1)}, u32[]{:S(2)}, u32[]{:S(2)}) %collective-permute-start.3) | collective-permute-done | bytes 786464 | tf_op jit(solution)/shard_map/ppermute | solution.py:19
  428.5 465.0 %all-reduce.2.cloned.1.call-done = f32[512,1024]{1,0:T(8,128)} async-done(((f32[512,1024]{1,0:T(8,128)}), f32[512,1024]{1,0:T(8,128)}) %all-reduce.2.cloned.1.call-update) | async-done | bytes 2097168 | tf_op jit(solution)/shard_map/psum | solution.py:124
  (206 shorter events, 130.9 us)
Async XLA Ops:
  7.2 146.9 %copy-start = (bf16[2,192,1024]{2,1,0:T(8,128)(2,1)S(1)}, bf16[2,192,1024]{2,1,0:T(8,128)(2,1)}, u32[]{:S(2)}) copy-start(bf16[2,192,1024]{2,1,0:T(8,128)(2,1)} %param.21) | copy-start | bytes 2359300
  7.2 55.9 %all-gather.8.cloned.1.call-start = ((), (), s32[]{:S(2)}) async-start(), calls=%async_computation.1 | async-start | bytes 1179648 | tf_op jit(solution)/shard_map/all_gather | solution.py:39
  7.9 99.4 %all-gather.6.cloned.1.call-start = ((), (), s32[]{:S(2)}) async-start(), calls=%async_computation | async-start | bytes 1179648 | tf_op jit(solution)/shard_map/all_gather | solution.py:38
  8.7 145.4 %all-gather.12.cloned.1.call-start = ((), (), s32[]{:S(2)}) async-start(), calls=%async_computation.3 | async-start | bytes 1179648 | tf_op jit(solution)/shard_map/all_gather | solution.py:40
  9.4 206.8 %all-gather.10.cloned.1.call-start = ((), (), s32[]{:S(2)}) async-start(), calls=%async_computation.2 | async-start | bytes 1179648 | tf_op jit(solution)/shard_map/all_gather | solution.py:37
  10.0 97.4 %copy-start.2 = (bf16[2,192,1024]{2,1,0:T(8,128)(2,1)S(1)}, bf16[2,192,1024]{2,1,0:T(8,128)(2,1)}, u32[]{:S(2)}) copy-start(bf16[2,192,1024]{2,1,0:T(8,128)(2,1)} %param.13) | copy-start | bytes 2359300
  10.0 883.5 %all-reduce.2.cloned.1.call-start = ((), (), s32[]{:S(2)}) async-start(), calls=%async_computation.4 | async-start | bytes 4194304 | tf_op jit(solution)/shard_map/psum | solution.py:124
  65.1 51.2 %copy-start.10 = (s32[3,9]{1,0:T(4,128)S(1)}, s32[3,9]{1,0:T(4,128)}, u32[]{:S(2)}) copy-start(s32[3,9]{1,0:T(4,128)} %param.20) | copy-start | bytes 328
  110.2 108.6 %collective-permute-start.1 = (bf16[2,192,1024]{2,1,0:T(8,128)(2,1)}, bf16[2,192,1024]{2,1,0:T(8,128)(2,1)S(1)}, u32[]{:S(2)}, u32[]{:S(2)}) collective-permute-start(bf16[2,192,1024]{2,1,0:T(8,128)(2,1)} %pad_maximum_fusion.1), channel_id=1, source_target_pairs={{8,0},{16,8},{24,16},{32,24},{40,32},{48,40},{56,48},{64,56},{72,6... | collective-permute-start | bytes 2359304 | tf_op jit(solution)/shard_map/ppermute | solution.py:19
  111.5 107.3 %collective-permute-start = (bf16[2,192,1024]{2,1,0:T(8,128)(2,1)}, bf16[2,192,1024]{2,1,0:T(8,128)(2,1)}, u32[]{:S(2)}, u32[]{:S(2)}) collective-permute-start(bf16[2,192,1024]{2,1,0:T(8,128)(2,1)} %pad_maximum_fusion.1), channel_id=1, source_target_pairs={{0,8},{8,16},{16,24},{24,32},{32,40},{40,48},{48,56},{56,64},{64,7... | collective-permute-start | bytes 2359304 | tf_op jit(solution)/shard_map/ppermute | solution.py:18
  281.2 7.7 copy-start.1
  311.6 7.7 copy-start.1
  342.0 7.7 copy-start.1
  372.5 7.7 copy-start.1
  386.8 3.5 copy-start.4
  400.0 7.2 copy-start.5
  401.0 21.0 %collective-permute-start.3 = (bf16[2,192,1024]{2,1,0:T(8,128)(2,1)}, bf16[2,192,1024]{2,1,0:T(8,128)(2,1)}, u32[]{:S(2)}, u32[]{:S(2)}) collective-permute-start(bf16[2,192,1024]{2,1,0:T(8,128)(2,1)} %get-tuple-element.247), channel_id=1, source_target_pairs={{8,0},{16,8},{24,16},{32,24},{40,32},{48,40},{56,48},{64,56},{72,6... | collective-permute-start | bytes 2359304 | tf_op jit(solution)/shard_map/ppermute | solution.py:19
  402.3 20.3 %collective-permute-start.2 = (bf16[2,192,1024]{2,1,0:T(8,128)(2,1)S(1)}, bf16[2,192,1024]{2,1,0:T(8,128)(2,1)}, u32[]{:S(2)}, u32[]{:S(2)}) collective-permute-start(bf16[2,192,1024]{2,1,0:T(8,128)(2,1)S(1)} %get-tuple-element.246), channel_id=1, source_target_pairs={{0,8},{8,16},{16,24},{24,32},{32,40},{40,48},{48,56},{56,64},{64,7... | collective-permute-start | bytes 2359304 | tf_op jit(solution)/shard_map/ppermute | solution.py:18
  409.3 2.8 copy-start.6
  409.3 2.8 copy-start.8
  412.7 12.2 %copy-start.7 = (bf16[1024,512]{1,0:T(8,128)(2,1)S(1)}, bf16[1024,512]{1,0:T(8,128)(2,1)}, u32[]{:S(2)}) copy-start(bf16[1024,512]{1,0:T(8,128)(2,1)} %all-gather.6.cloned.1.call-done) | copy-start | bytes 3145732
  424.9 1.1 copy-start.3
  424.9 1.5 copy-start.9
Sparse Core Ops, SparseCore 0:
  10.1 52.8 all-gather.7
  65.2 42.0 all-gather.5
  109.5 44.4 all-gather.11
  156.0 60.1 all-gather.9
  409.4 484.0 all-reduce.1
where the time goes:
time: 903 us; the launch traced here: 902 us
  waiting for transfers between devices  645 us (71%)
  matrix products  106 us (12%)
  local copies, waits for them, and re-layouts  73.6 us (8%)
  blocking collectives  22.8 us (3%)
  other arithmetic  22.2 us (2%)
  between operations  14 us (2%)
  starting transfers between devices  12.5 us (1%)
    psum x1, waiting for transfers between devices, shards(): total_grad = lax.psum(incomplete_gradient, ('domain', 'member'))  465 us
    all_gather x1, waiting for transfers between devices, shards(): lax.all_gather(w_query, 'member', axis=0, tiled=True)  59.6 us
    all_gather x1, waiting for transfers between devices, shards(): lax.all_gather(w_key, 'member', axis=0, tiled=True)  42.2 us
    all_gather x1, waiting for transfers between devices, shards(): lax.all_gather(w_out, 'member', axis=0, tiled=True)  37.4 us
    dot_general x4, matrix products, backward_pair(): jnp.einsum(mix_spec, d_score, key_pair, preferred_element_type=jnp.float32)  31.3 us
    dot_general x4, matrix products, backward_pair(): jnp.einsum(back_spec, d_score, query_pair, preferred_element_type=jnp.flo...  30.7 us
    all_gather x1, waiting for transfers between devices, shards(): lax.all_gather(w_value, 'member', axis=0, tiled=True)  28.1 us
    dynamic_slice x24, local copies, waits for them, and re-layouts, pair_columns(): lax.dynamic_slice_in_dim(field, pair_index * pair_width, pair_width, fiel...  23.5 us
  transfers between devices with their start and end apart: 9, of which 7 were waited for; matrix products, arithmetic and copies ran while one was open for 3% of the time, Pallas kernels for 0%

commit v1 on v0

--- a/solution.py
+++ b/solution.py
@@ -35,7 +35,9 @@
     full_gain, complete_query, complete_key, complete_value, complete_output = (
         lax.all_gather(norm_gain, "member", axis=0, tiled=True),
         lax.all_gather(w_query, "member", axis=0, tiled=True),
-        lax.all_gather(w_key, "member", axis=0, tiled=True),
+        jnp.concatenate(
+            lax.all_to_all(jnp.stack([w_key] * lax.axis_size("member")), "member", 0, 0), axis=0
+        ),
         lax.all_gather(w_value, "member", axis=0, tiled=True),
         lax.all_gather(w_out, "member", axis=0, tiled=True),
     )

time: 903 us -> 899 us (level)
  waiting for transfers between devices: 645 us -> 582 us
  blocking collectives: 22.8 us -> 67.3 us
  starting transfers between devices: 12.5 us -> 28.2 us
    all_gather x1, blocking collectives: 22.8 us -> 67.3 us  [shards(): lax.all_gather(norm_gain, 'member', axis=0, tiled=True)]
    all_gather x1 -> x0, waiting for transfers between devices: 42.2 us -> none  [shards(): lax.all_gather(w_key, 'member', axis=0, tiled=True)]
    all_gather x1, waiting for transfers between devices: 28.1 us -> 2.62 us  [shards(): lax.all_gather(w_value, 'member', axis=0, tiled=True)]
    all_to_all x0 -> x1, starting transfers between devices: none -> 16.6 us  [shards(): lax.all_to_all(jnp.stack([w_key] * lax.axis_size('member')), 'member', 0, 0)]
  transfers between devices with their start and end apart: 9 -> 9, of which waited for: 7 -> 6; matrix products, arithmetic and copies ran while one was open for 3% -> 2% of each run, Pallas kernels for 0% -> 0%
where the time goes in v1:
time: 899 us; the launch traced here: 898 us
  waiting for transfers between devices  582 us (65%)
  matrix products  105 us (12%)
  local copies, waits for them, and re-layouts  75.7 us (8%)
  blocking collectives  67.3 us (7%)
  starting transfers between devices  28.2 us (3%)
  other arithmetic  20.3 us (2%)
  between operations  14 us (2%)
    psum x1, waiting for transfers between devices, shards(): total_grad = lax.psum(incomplete_gradient, ('domain', 'member'))  465 us
    all_gather x1, blocking collectives, shards(): lax.all_gather(norm_gain, 'member', axis=0, tiled=True)  67.3 us
    all_gather x1, waiting for transfers between devices, shards(): lax.all_gather(w_query, 'member', axis=0, tiled=True)  64.4 us
    all_gather x1, waiting for transfers between devices, shards(): lax.all_gather(w_out, 'member', axis=0, tiled=True)  37.4 us
    dot_general x4, matrix products, backward_pair(): jnp.einsum(mix_spec, d_score, key_pair, preferred_element_type=jnp.float32)  31.3 us
    dot_general x4, matrix products, backward_pair(): jnp.einsum(back_spec, d_score, query_pair, preferred_element_type=jnp.flo...  30.7 us
    dynamic_slice x24, local copies, waits for them, and re-layouts, pair_columns(): lax.dynamic_slice_in_dim(field, pair_index * pair_width, pair_width, fiel...  23.5 us
  transfers between devices with their start and end apart: 9, of which 6 were waited for; matrix products, arithmetic and copies ran while one was open for 2% of the time, Pallas kernels for 0%

profile of v1, /device:TPU:1, one launch (start us, length us, event | category | flops | bytes accessed | tf_op | source)
XLA Modules:
  0.0 897.7 jit_solution(2861220251312943029)
XLA Ops:
  10.0 16.6 %all-to-all-start = ((bf16[8,128,512]{2,1,0:T(8,128)(2,1)}), bf16[8,128,512]{2,1,0:T(8,128)(2,1)S(1)}, u32[]{:S(2)}, u32[]{:S(2)}) async-start(bf16[8,128,512]{2,1,0:T(8,128)(2,1)} %stack.2), calls=%async_computation | async-start | bytes 2097152 | tf_op jit(solution)/shard_map/all_to_all | solution.py:39
  28.3 67.3 %all-gather = bf16[8,1,128]{2,1,0:T(2,128)(2,1)S(1)} all-gather(bf16[1,1,128]{2,1,0:T(2,128)(2,1)S(1)} %bitcast.207), channel_id=1, replica_groups=mesh['domain'=64,'member'=8] {'member'}, dimensions={0}, use_global_device_ids=true | all-gather | bytes 2304 | tf_op jit(solution)/shard_map/all_gather | solution.py:36
  95.6 2.6 all-gather.5.cloned.1.call-done
  103.0 4.0 collective-permute-start
  107.4 37.4 %all-gather.9.cloned.1.call-done = bf16[512,1024]{1,0:T(8,128)(2,1)} async-done(((bf16[64,1024]{1,0:T(8,128)(2,1)}), bf16[512,1024]{1,0:T(8,128)(2,1)}) %all-gather.9.cloned.1.call-update) | async-done | bytes 1048592 | tf_op jit(solution)/shard_map/all_gather | solution.py:42
  147.4 64.4 %all-gather.7.cloned.1.call-done = bf16[1024,512]{1,0:T(8,128)(2,1)} async-done(((bf16[128,512]{1,0:T(8,128)(2,1)}), bf16[1024,512]{1,0:T(8,128)(2,1)}) %all-gather.7.cloned.1.call-update) | async-done | bytes 1048592 | tf_op jit(solution)/shard_map/all_gather | solution.py:37
  219.8 34.7 %while.26 = (s32[]{:T(128)}, bf16[4,2,192,128]{3,2,1,0:T(8,128)(2,1)}, s32[4]{0:T(128)S(1)}, bf16[2,576,512]{1,2,0:T(8,128)(2,1)}, bf16[2,576,512]{1,2,0:T(8,128...) while((s32[]{:T(128)}, ...), condition=%wide.region_5.6_spmd.clone, body=%wide.region_2.5_spmd.clone.sunk | while | flops 117278592 | bytes 8469142 | solution.py:111
  255.3 121.7 %while.27 = (s32[]{:T(128)}, bf16[4,2,192,128]{3,2,1,0:T(8,128)(2,1)}, f32[4,2,576,128]{2,3,1,0:T(8,128)}, f32[4,2,576,128]{2,3,1,0:T(8,128)}, s32[4]{0:T(128)S(...) while((s32[]{:T(128)}, ...), condition=%wide.region_10.11_spmd.clone, body=%wide.region_6.0_spmd.clone.sunk | while | flops 293343744 | bytes 26301140 | solution.py:147
  264.7 7.8 fusion.143
  276.8 7.7 fusion.145
  295.1 7.8 fusion.143
  307.2 7.7 fusion.145
  325.5 7.8 fusion.143
  337.6 7.7 fusion.145
  356.0 7.8 fusion.143
  368.1 7.7 fusion.145
  377.0 3.2 copy.65
  382.3 3.5 constant_dynamic-update-slice_fusion.5
  388.4 2.7 reshape.88
  392.8 2.7 convert.6
  397.9 4.9 collective-permute-start.2
  404.9 2.8 convolution_convert_fusion.1
  408.3 9.3 %collective-permute-done.3 = bf16[2,192,1024]{2,1,0:T(8,128)(2,1)} collective-permute-done((bf16[2,192,1024]{2,1,0:T(8,128)(2,1)}, bf16[2,192,1024]{2,1,0:T(8,128)(2,1)}, u32[]{:S(2)}, u32[]{:S(2)}) %collective-permute-start.3) | collective-permute-done | bytes 786464 | tf_op jit(solution)/shard_map/ppermute | solution.py:19
  424.0 465.5 %all-reduce.2.cloned.1.call-done = f32[512,1024]{1,0:T(8,128)} async-done(((f32[512,1024]{1,0:T(8,128)}), f32[512,1024]{1,0:T(8,128)}) %all-reduce.2.cloned.1.call-update) | async-done | bytes 2097168 | tf_op jit(solution)/shard_map/psum | solution.py:126
  (212 shorter events, 129.0 us)
Async XLA Ops:
  7.2 137.7 %copy-start = (bf16[2,192,1024]{2,1,0:T(8,128)(2,1)S(1)}, bf16[2,192,1024]{2,1,0:T(8,128)(2,1)}, u32[]{:S(2)}) copy-start(bf16[2,192,1024]{2,1,0:T(8,128)(2,1)} %param.21) | copy-start | bytes 2359300
  7.2 20.9 %copy-start.2 = (bf16[2,192,1024]{2,1,0:T(8,128)(2,1)S(1)}, bf16[2,192,1024]{2,1,0:T(8,128)(2,1)}, u32[]{:S(2)}) copy-start(bf16[2,192,1024]{2,1,0:T(8,128)(2,1)} %param.13) | copy-start | bytes 2359300
  7.2 91.1 %all-gather.5.cloned.1.call-start = ((), (), s32[]{:S(2)}) async-start(), calls=%async_computation.1 | async-start | bytes 1179648 | tf_op jit(solution)/shard_map/all_gather | solution.py:41
  7.9 20.4 %copy-start.13 = (bf16[128]{0:T(256)(128)(2,1)S(1)}, bf16[128]{0:T(256)(128)(2,1)}, u32[]{:S(2)}) copy-start(bf16[128]{0:T(256)(128)(2,1)} %param.14) | copy-start | bytes 772
  7.9 87.7 %copy-start.12 = (s32[3,9]{1,0:T(4,128)S(1)}, s32[3,9]{1,0:T(4,128)}, u32[]{:S(2)}) copy-start(s32[3,9]{1,0:T(4,128)} %param.19) | copy-start | bytes 328
  10.0 90.1 %all-to-all-start = ((bf16[8,128,512]{2,1,0:T(8,128)(2,1)}), bf16[8,128,512]{2,1,0:T(8,128)(2,1)S(1)}, u32[]{:S(2)}, u32[]{:S(2)}) async-start(bf16[8,128,512]{2,1,0:T(8,128)(2,1)} %stack.2), calls=%async_computation | async-start | bytes 2097152 | tf_op jit(solution)/shard_map/all_to_all | solution.py:39
  26.6 118.3 %all-gather.9.cloned.1.call-start = ((), (), s32[]{:S(2)}) async-start(), calls=%async_computation.3 | async-start | bytes 1179648 | tf_op jit(solution)/shard_map/all_gather | solution.py:42
  27.3 184.5 %all-gather.7.cloned.1.call-start = ((), (), s32[]{:S(2)}) async-start(), calls=%async_computation.2 | async-start | bytes 1179648 | tf_op jit(solution)/shard_map/all_gather | solution.py:37
  28.0 861.5 %all-reduce.2.cloned.1.call-start = ((), (), s32[]{:S(2)}) async-start(), calls=%async_computation.4 | async-start | bytes 4194304 | tf_op jit(solution)/shard_map/psum | solution.py:126
  100.1 1.6 copy-start.4
  100.1 7.0 copy-start.11
  101.7 112.6 %collective-permute-start.1 = (bf16[2,192,1024]{2,1,0:T(8,128)(2,1)}, bf16[2,192,1024]{2,1,0:T(8,128)(2,1)}, u32[]{:S(2)}, u32[]{:S(2)}) collective-permute-start(bf16[2,192,1024]{2,1,0:T(8,128)(2,1)} %pad_maximum_fusion.1), channel_id=1, source_target_pairs={{8,0},{16,8},{24,16},{32,24},{40,32},{48,40},{56,48},{64,56},{72,6... | collective-permute-start | bytes 2359304 | tf_op jit(solution)/shard_map/ppermute | solution.py:19
  103.0 111.4 %collective-permute-start = (bf16[2,192,1024]{2,1,0:T(8,128)(2,1)}, bf16[2,192,1024]{2,1,0:T(8,128)(2,1)S(1)}, u32[]{:S(2)}, u32[]{:S(2)}) collective-permute-start(bf16[2,192,1024]{2,1,0:T(8,128)(2,1)} %pad_maximum_fusion.1), channel_id=1, source_target_pairs={{0,8},{8,16},{16,24},{24,32},{32,40},{40,48},{48,56},{56,64},{64,7... | collective-permute-start | bytes 2359304 | tf_op jit(solution)/shard_map/ppermute | solution.py:18
  276.8 7.7 copy-start.1
  307.2 7.7 copy-start.1
  337.6 7.7 copy-start.1
  368.1 7.7 copy-start.1
  382.3 3.5 copy-start.6
  395.5 7.2 copy-start.7
  396.6 21.0 %collective-permute-start.3 = (bf16[2,192,1024]{2,1,0:T(8,128)(2,1)}, bf16[2,192,1024]{2,1,0:T(8,128)(2,1)}, u32[]{:S(2)}, u32[]{:S(2)}) collective-permute-start(bf16[2,192,1024]{2,1,0:T(8,128)(2,1)} %get-tuple-element.247), channel_id=1, source_target_pairs={{8,0},{16,8},{24,16},{32,24},{40,32},{48,40},{56,48},{64,56},{72,6... | collective-permute-start | bytes 2359304 | tf_op jit(solution)/shard_map/ppermute | solution.py:19
  397.9 20.3 %collective-permute-start.2 = (bf16[2,192,1024]{2,1,0:T(8,128)(2,1)S(1)}, bf16[2,192,1024]{2,1,0:T(8,128)(2,1)}, u32[]{:S(2)}, u32[]{:S(2)}) collective-permute-start(bf16[2,192,1024]{2,1,0:T(8,128)(2,1)S(1)} %get-tuple-element.246), channel_id=1, source_target_pairs={{0,8},{8,16},{16,24},{24,32},{32,40},{40,48},{48,56},{56,64},{64,7... | collective-permute-start | bytes 2359304 | tf_op jit(solution)/shard_map/ppermute | solution.py:18
  404.8 2.8 copy-start.8
  404.8 2.8 copy-start.9
  408.3 12.2 %copy-start.5 = (bf16[8,128,512]{2,1,0:T(8,128)(2,1)S(1)}, bf16[8,128,512]{2,1,0:T(8,128)(2,1)}, u32[]{:S(2)}) copy-start(bf16[8,128,512]{2,1,0:T(8,128)(2,1)} %copy-done.4) | copy-start | bytes 3145732
  (2 other events, 2.6 us)
Sparse Core Ops, SparseCore 0:
  10.2 88.0 all-gather.4
  100.4 44.3 all-gather.8
  147.0 64.7 all-gather.6
  405.0 484.4 all-reduce.1
